TPU v7x, 256 devices: a whole 4x4x8 slice. The times are simulated.
256 devices in a mesh: grp: 2 (over core), dom: 64 (over y_lo, z, x), sub: 2 (over y_hi).
Axes of the slice: x: 4, y: 4 (y_hi: 2, y_lo: 2; y = y_hi * 2 + y_lo), z: 8, core: 2. Of those that a mesh axis runs over, the one named last changes fastest.
Arguments:
- positions: float32 [3, 65536], P(None, ('grp', 'dom', 'sub')), may hold values from 0 to 4
- charges: float32 [65536], P(('grp', 'dom', 'sub')), may hold values from -3 to 3
- polar: float32 [65536], P(('grp', 'dom', 'sub')), may hold values from 0.1 to 0.6
- features: bfloat16 [65536, 256], P(('grp', 'dom', 'sub')), may hold values from -6 to 6
- neighbours: int32 [65536, 32], P(('grp', 'dom', 'sub')), may hold values from 0 to 512, as said below
- send_rows: int32 [2, 32768], P(None, ('grp', 'dom', 'sub')), may hold values from 0 to 255
- blocks: int32 [1024], P(('grp', 'dom', 'sub')), may hold values from 0 to 255
- radial_in: bfloat16 [2, 8, 64], replicated, may hold values from -2 to 2
- radial_mid: bfloat16 [2, 2, 64, 64], replicated, may hold values from -0.75 to 0.75
- radial_out: bfloat16 [2, 64, 256], replicated, may hold values from -0.75 to 0.75
- node_in: bfloat16 [2, 256, 256], replicated, may hold values from -0.375 to 0.375
- node_out: bfloat16 [2, 256, 256], replicated, may hold values from -0.375 to 0.375
- field_gain: float32 [256], replicated, may hold values from -3 to 3
- readout: bfloat16 [256, 2], replicated, may hold values from -0.375 to 0.375
Outputs:
- site_result: float32 [3, 65536], P(None, ('grp', 'dom', 'sub'))
- response: float32 [3, 65536], P(None, ('grp', 'dom', 'sub'))
Inputs may be any that keep to these rules, and one draw needn't show every extreme that they name: `neighbours`: entries below 256 name the block's own sites, entries from 256 to 511 its lent sites, 512 an empty slot; empty slots follow the used ones. `blocks`: repeats may occur.
All inputs are finite; a program needn't handle non-finite values.
Results may differ from a plain program's by a relative error of at most 0.0022.
The roundings to bfloat16 on the way count: a program that leaves them out, or rounds other values in their place, can miss the bound.
Values may be sent and summed in bfloat16 or wider, within the bound.
No kernel may reach another device: no remote copies, remote signals or barrier semaphores. Data moves between devices by JAX's collectives and lax.ppermute only.
A program may use at most 64 MiB of HBM per device.

v0:
```python
import jax
import jax.numpy as jnp
from jax import lax
from jax.sharding import PartitionSpec as P

BASIS = 8
LAYERS = 2
SWEEPS = 4
BLOCK = 128
SMOOTH = 1.0
GAMMA = 1.0
SPACING = 0.75


def with_halo(block, sides, width):
    for axis, dim in sides:
        count = lax.axis_size(axis)
        forward = [(i, i + 1) for i in range(count - 1)]
        backward = [(target, source) for source, target in forward]
        low = lax.ppermute(
            lax.slice_in_dim(block, block.shape[dim] - width, None, axis=dim), axis, forward
        )
        high = lax.ppermute(lax.slice_in_dim(block, 0, width, axis=dim), axis, backward)
        block = jnp.concatenate([low, block, high], axis=dim)
    return block


def partner_2(value, axis, bit):
    mask = 2**bit
    pairs = [(source, source ^ mask) for source in range(lax.axis_size(axis))]
    return lax.ppermute(value, axis, pairs)


def field_at(target, source, charge, dipole):
    tile_count = target.shape[1] // BLOCK
    tiles = target.reshape(3, tile_count, BLOCK).transpose(1, 0, 2)

    def field_one_tile(target_tile):
        offset = target_tile[:, :, None] - source[:, None, :]
        dist_sq = jnp.sum(offset * offset, axis=0) + SMOOTH
        inverse = lax.rsqrt(dist_sq)
        inverse_cube = inverse * inverse * inverse
        inverse_fifth = inverse_cube * inverse * inverse
        projected = jnp.sum(offset * dipole[:, None, :], axis=0)
        source_scale = charge[None, :] * inverse_cube + 3.0 * projected * inverse_fifth
        return jnp.sum(
            offset * source_scale[None] - dipole[:, None, :] * inverse_cube[None], axis=2
        )

    return lax.map(field_one_tile, tiles).transpose(1, 0, 2).reshape(3, -1)


def slot_field(offset, dist_sq, source_charge, source_dipole):
    inverse = lax.rsqrt(dist_sq)
    inverse_cube = inverse * inverse * inverse
    inverse_fifth = inverse_cube * inverse * inverse
    projected = jnp.sum(offset * source_dipole, axis=0)
    source_scale = source_charge * inverse_cube + 3.0 * projected * inverse_fifth
    return jnp.sum(offset * source_scale[None] - source_dipole * inverse_cube[None], axis=1)


def message_update(
    hidden, lifted_table, radial_basis, slot_major, w_first, w_middle, w_last, w_node
):
    row_count, channel_count = hidden.shape
    slot_count = slot_major.shape[0]
    basis_width = radial_basis.shape[2]
    tile_count = row_count // BLOCK

    def message_one_tile(tile_index):
        start = tile_index * BLOCK
        basis_tile = lax.dynamic_slice_in_dim(radial_basis, start, BLOCK, 1).reshape(
            slot_count * BLOCK, basis_width
        )
        index_tile = lax.dynamic_slice_in_dim(slot_major, start, BLOCK, 1)
        first_hidden = jax.nn.silu(
            jnp.dot(basis_tile, w_first, preferred_element_type=jnp.float32)
        ).astype(jnp.bfloat16)
        second_hidden = jax.nn.silu(
            jnp.dot(first_hidden, w_middle[0], preferred_element_type=jnp.float32)
        ).astype(jnp.bfloat16)
        third_hidden = jax.nn.silu(
            jnp.dot(second_hidden, w_middle[1], preferred_element_type=jnp.float32)
        ).astype(jnp.bfloat16)
        edge_weight = jnp.dot(third_hidden, w_last, preferred_element_type=jnp.float32).reshape(
            slot_count, BLOCK, channel_count
        )
        source = lifted_table[index_tile].astype(jnp.float32)
        summed = jnp.sum(edge_weight * source, axis=0)
        return summed / slot_count

    message = (
        lax.map(message_one_tile, jnp.arange(tile_count, dtype=jnp.int32))
        .reshape(row_count, channel_count)
        .astype(jnp.bfloat16)
    )
    update = jax.nn.silu(jnp.dot(message, w_node, preferred_element_type=jnp.float32))
    return (hidden.astype(jnp.float32) + update).astype(jnp.bfloat16)


def extend_cols(values, rim_rows, rim_width):
    empty_entry = jnp.zeros(values.shape[:-1] + (1,), values.dtype)
    return jnp.concatenate(
        [values, rim_rows[..., :rim_width], rim_rows[..., 3 * rim_width :], empty_entry], axis=-1
    )


def extend_rows(values, rim_rows, rim_width):
    empty_entry = jnp.zeros((1,) + values.shape[1:], values.dtype)
    return jnp.concatenate(
        [values, rim_rows[:rim_width], rim_rows[3 * rim_width :], empty_entry], axis=0
    )


def local(
    positions,
    charges,
    polar,
    features,
    neighbours,
    send_rows,
    blocks,
    radial_in,
    radial_mid,
    radial_out,
    node_in,
    node_out,
    field_gain,
    readout,
):
    rim_width = send_rows.shape[1]
    row_count = positions.shape[1]
    block_width = BLOCK
    own_blocks = row_count // block_width
    listed_count = blocks.shape[0]
    domain_count = lax.axis_size(("dom", "sub"))
    domain_index = lax.axis_index(("dom", "sub"))
    group_blocks = own_blocks * domain_count
    learned = lax.axis_index("grp") == 0
    slot_major = neighbours.T
    local_data = jnp.concatenate([positions, charges[None], polar[None]], axis=0)
    outgoing = jnp.concatenate([local_data[:, send_rows[1]], local_data[:, send_rows[0]]], axis=1)
    rim_rows = with_halo(outgoing, ((("dom", "sub"), 1),), rim_width)
    site_table = extend_cols(local_data, rim_rows, rim_width)
    partner = partner_2(local_data, "grp", 0)
    others = lax.all_gather(partner, ("dom", "sub"), axis=1, tiled=True)
    near_sites = jnp.take(others.reshape(5, -1, block_width), blocks, axis=1).reshape(5, -1)
    outside = field_at(positions, near_sites[:3], near_sites[3], jnp.zeros_like(near_sites[:3]))
    offset = positions[:, None, :] - site_table[:3][:, slot_major]
    dist_sq = jnp.sum(offset * offset, axis=0) + SMOOTH
    strength = jnp.sqrt(1.0 + jnp.sum(outside * outside, axis=0))
    hidden = (features.astype(jnp.float32) + strength[:, None] * field_gain[None, :]).astype(
        jnp.bfloat16
    )
    centres = jnp.arange(BASIS, dtype=jnp.float32) * SPACING
    radial_basis = jnp.exp(-GAMMA * (jnp.sqrt(dist_sq)[:, :, None] - centres) ** 2).astype(
        jnp.bfloat16
    )
    for layer_index in range(LAYERS):
        lifted = lax.cond(
            learned,
            lambda h: jnp.dot(h, node_in[layer_index], preferred_element_type=jnp.float32).astype(
                jnp.bfloat16
            ),
            lambda h: jnp.zeros_like(h),
            hidden,
        )
        lent = jnp.concatenate([lifted[send_rows[1]], lifted[send_rows[0]]], axis=0)
        lifted_rims = with_halo(lent, ((("dom", "sub"), 0),), rim_width)
        lifted_table = extend_rows(lifted, lifted_rims, rim_width)
        hidden = lax.cond(
            learned,
            lambda h, t: message_update(
                h,
                t,
                radial_basis,
                slot_major,
                radial_in[layer_index],
                radial_mid[layer_index],
                radial_out[layer_index],
                node_out[layer_index],
            ),
            lambda h, t: h,
            hidden,
            lifted_table,
        )
    readouts = jnp.dot(hidden, readout, preferred_element_type=jnp.float32)
    charge = readouts[:, 0]
    energy = readouts[:, 1]
    fixed_field = outside + slot_field(
        offset, dist_sq, site_table[3][slot_major], jnp.zeros_like(offset)
    )
    dipole = jnp.where(learned, 0.0, polar[None] * fixed_field)
    for sweep_index in range(SWEEPS):
        lent_dipoles = jnp.concatenate([dipole[:, send_rows[1]], dipole[:, send_rows[0]]], axis=1)
        dipole_rims = with_halo(lent_dipoles, ((("dom", "sub"), 1),), rim_width)
        dipole_table = extend_cols(dipole, dipole_rims, rim_width)
        dipole = lax.cond(
            learned,
            lambda d, t: d,
            lambda d, t: polar[None]
            * (
                fixed_field + slot_field(offset, dist_sq, jnp.zeros_like(dist_sq), t[:, slot_major])
            ),
            dipole,
            dipole_table,
        )
    site_result = jnp.where(learned, jnp.stack([charge, energy, strength]), dipole)
    source_charge = jnp.where(learned, charge, 0.0)
    source_dipole = jnp.where(learned, 0.0, dipole)
    response_term = field_at(near_sites[:3], positions, source_charge, source_dipole)
    scattered = (
        jnp.zeros((3, group_blocks, block_width), jnp.float32)
        .at[:, blocks]
        .add(response_term.reshape(3, listed_count, block_width))
        .reshape(3, -1)
    )
    total = lax.psum(scattered, ("dom", "sub"))
    own_share = lax.dynamic_slice_in_dim(total, domain_index * row_count, row_count, 1)
    response = partner_2(own_share, "grp", 0)
    return (site_result, response)


def solution(mesh):
    in_specs = (
        P(None, ("grp", "dom", "sub")),
        P(("grp", "dom", "sub")),
        P(("grp", "dom", "sub")),
        P(("grp", "dom", "sub"), None),
        P(("grp", "dom", "sub"), None),
        P(None, ("grp", "dom", "sub")),
        P(("grp", "dom", "sub")),
        P(),
        P(),
        P(),
        P(),
        P(),
        P(),
        P(),
    )
    out_specs = (P(None, ("grp", "dom", "sub")), P(None, ("grp", "dom", "sub")))
    return jax.shard_map(local, mesh=mesh, in_specs=in_specs, out_specs=out_specs, check_vma=False)
```

profile of v0, /device:TPU:1, one launch (start us, length us, event | category | flops | bytes accessed | tf_op | source)
XLA Modules:
  0.0 878.2 jit_solution(3538958461297963734)
XLA Ops:
  8.0 3.2 collective-permute-start
  14.7 5.5 collective-permute-start.1
  24.2 32.9 %gather_fusion.14 = f32[8192]{0:T(1024)S(1)} fusion(f32[513]{0:T(1024)S(1)} %slice_reduce_fusion, s32[8192]{0:T(1024)S(1)} %broadcast_clamp_fusion.4), kind=kCustom, calls=%fused_computation.14 | custom fusion | bytes 98304 | tf_op jit(solution)/shard_map/gather | solution.py:191
  57.2 27.9 %gather_fusion.9 = f32[8192,3]{1,0:T(8,128)} fusion(f32[3,513]{0,1:T(8,128)S(1)} %copy.124, s32[8192]{0:T(1024)S(1)} %broadcast_clamp_fusion.4), kind=kCustom, calls=%fused_computation.9 | custom fusion | bytes 229376 | tf_op jit(solution)/shard_map/gather | solution.py:149
  85.1 4.5 multiply_reduce_fusion.4
  89.6 1.9 copy-done.1
  91.5 2.5 subtract_reduce_fusion.4
  94.0 296.4 %all_gather.3 = f32[5,32768]{1,0:T(8,128)S(1)} all-gather(f32[5,256]{1,0:T(8,128)S(1)} %collective-permute-done), channel_id=1, replica_groups=mesh['grp'=2,'dom'=64,'sub'=2] {'dom','sub'}, dimensions={1}, use_global_device_ids=true | all-gather | bytes 660480 | tf_op jit(solution)/shard_map/all_gather | solution.py:146
  395.2 5.5 collective-permute-start.7
  402.1 36.6 %conditional.12 = (f32[3,256]{0,1:T(8,128)S(1)}) conditional(s32[]{:T(128)} %convert_element_type.76, (f32[256]{0:T(256)S(1)}, f32[32,256]{1,0:T(8,128)S(1)}, s32[32,256]{1,0:T(8,128)S(1)}, f32[3,513]{1,0:T(4,128)S(1)}, f32[3,32,256]{0,2,1:T(8,128)}, /*index=5*/f32[3,256]{0,1:T(8,128)S(1)}) %tuple.225, f32[3,256]{0,1:T(8,128)S(1)} %get-tuple-element.543), branch_computations={%region_23.26_spmd, %region_26.27_spmd} | conditional | flops 238336 | bytes 1860696 | solution.py:198
  402.3 27.9 %gather_fusion = f32[8192,3]{1,0:T(8,128)} fusion(f32[3,513]{0,1:T(8,128)S(1)} %copy.129, s32[8192]{0:T(1024)S(1)} %broadcast_clamp_fusion), kind=kCustom, calls=%fused_computation.2 | custom fusion | bytes 229376 | tf_op jit(solution)/shard_map/cond/branch_0_fun/gather | solution.py:203
  430.2 4.8 multiply_reduce_fusion
  436.1 2.5 subtract_reduce_fusion
  441.3 6.1 collective-permute-start.9
  448.9 36.7 %conditional.13 = (f32[3,256]{0,1:T(8,128)S(1)}) conditional(s32[]{:T(128)} %convert_element_type.76, (f32[256]{0:T(256)S(1)}, f32[32,256]{1,0:T(8,128)S(1)}, s32[32,256]{1,0:T(8,128)S(1)}, f32[3,513]{1,0:T(4,128)S(1)}, f32[3,32,256]{0,2,1:T(8,128)}, /*index=5*/f32[3,256]{0,1:T(8,128)S(1)}) %tuple.226, f32[3,256]{0,1:T(8,128)S(1)} %get-tuple-element.898), branch_computations={%region_27.30_spmd, %region_30.31_spmd} | conditional | flops 238336 | bytes 1860696 | solution.py:198
  449.1 27.9 %gather_fusion.1 = f32[8192,3]{1,0:T(8,128)} fusion(f32[3,513]{0,1:T(8,128)S(1)} %copy.133, s32[8192]{0:T(1024)S(1)} %broadcast_clamp_fusion.1), kind=kCustom, calls=%fused_computation.3 | custom fusion | bytes 229376 | tf_op jit(solution)/shard_map/cond/branch_0_fun/gather | solution.py:203
  477.0 4.8 multiply_reduce_fusion.1
  482.9 2.5 subtract_reduce_fusion.1
  488.1 6.4 collective-permute-start.11
  497.9 6.7 collective-permute-start.3
  504.9 36.6 %conditional.14 = (f32[3,256]{0,1:T(8,128)S(1)}) conditional(s32[]{:T(128)} %convert_element_type.76, (f32[256]{0:T(256)S(1)}, f32[32,256]{1,0:T(8,128)S(1)}, s32[32,256]{1,0:T(8,128)S(1)}, f32[3,513]{1,0:T(4,128)S(1)}, f32[3,32,256]{0,2,1:T(8,128)}, /*index=5*/f32[3,256]{0,1:T(8,128)S(1)}) %tuple.227, f32[3,256]{0,1:T(8,128)S(1)} %get-tuple-element.899), branch_computations={%region_31.34_spmd, %region_34.35_spmd} | conditional | flops 238336 | bytes 1860696 | solution.py:198
  505.1 27.9 %gather_fusion.2 = f32[8192,3]{1,0:T(8,128)} fusion(f32[3,513]{0,1:T(8,128)S(1)} %copy.137, s32[8192]{0:T(1024)S(1)} %broadcast_clamp_fusion.2), kind=kCustom, calls=%fused_computation.4 | custom fusion | bytes 229376 | tf_op jit(solution)/shard_map/cond/branch_0_fun/gather | solution.py:203
  533.0 4.8 multiply_reduce_fusion.2
  538.9 2.5 subtract_reduce_fusion.2
  544.1 6.4 collective-permute-start.13
  555.2 6.4 collective-permute-start.5
  561.6 36.6 %conditional.15 = (f32[3,256]{0,1:T(8,128)S(1)}) conditional(s32[]{:T(128)} %convert_element_type.76, (f32[256]{0:T(256)S(1)}, f32[32,256]{1,0:T(8,128)S(1)}, s32[32,256]{1,0:T(8,128)S(1)}, f32[3,513]{1,0:T(4,128)S(1)}, f32[3,32,256]{0,2,1:T(8,128)}, /*index=5*/f32[3,256]{0,1:T(8,128)S(1)}) %tuple.228, f32[3,256]{0,1:T(8,128)S(1)} %get-tuple-element.900), branch_computations={%region_35.38_spmd, %region_38.39_spmd} | conditional | flops 238336 | bytes 1860696 | solution.py:198
  561.8 27.9 %gather_fusion.3 = f32[8192,3]{1,0:T(8,128)} fusion(f32[3,513]{0,1:T(8,128)S(1)} %copy.141, s32[8192]{0:T(1024)S(1)} %broadcast_clamp_fusion.3), kind=kCustom, calls=%fused_computation.5 | custom fusion | bytes 229376 | tf_op jit(solution)/shard_map/cond/branch_0_fun/gather | solution.py:203
  589.7 4.8 multiply_reduce_fusion.3
  595.6 2.5 subtract_reduce_fusion.3
  602.6 261.5 %all-reduce.2.cloned.1.call-done = f32[3,32768]{1,0:T(4,128)} async-done(((f32[3,32768]{1,0:T(4,128)}), f32[3,32768]{1,0:T(4,128)}) %all-reduce.2.cloned.1.call-update) | async-done | bytes 393232 | tf_op jit(solution)/shard_map/psum | solution.py:218
  864.8 5.2 collective-permute-start.15
  (210 shorter events, 46.6 us)
Async XLA Ops:
  7.2 591.5 %copy-start = (bf16[256,2]{0,1:T(2,128)(2,1)S(1)}, bf16[256,2]{0,1:T(2,128)(2,1)}, u32[]{:S(2)}) copy-start(bf16[256,2]{0,1:T(2,128)(2,1)} %param.51) | copy-start | bytes 3076
  7.2 856.9 %all-reduce.2.cloned.1.call-start = ((), (), s32[]{:S(2)}) async-start(), calls=%async_computation | async-start | bytes 1048576 | tf_op jit(solution)/shard_map/psum | solution.py:218
  8.0 86.1 %collective-permute-start = (f32[5,256]{1,0:T(8,128)S(1)}, f32[5,256]{1,0:T(8,128)S(1)}, u32[]{:S(2)}, u32[]{:S(2)}) collective-permute-start(f32[5,256]{1,0:T(8,128)S(1)} %pad_maximum_fusion), channel_id=1, source_target_pairs={{0,128},{128,0},{1,129},{129,1},{2,130},{130,2},{3,131},{131,3},{4... | collective-permute-start | bytes 15368 | tf_op jit(solution)/shard_map/ppermute | solution.py:31
  12.8 10.5 %collective-permute-start.2 = (f32[5,128]{0,1:T(8,128)S(1)}, f32[5,128]{0,1:T(8,128)S(1)}, u32[]{:S(2)}, u32[]{:S(2)}) collective-permute-start(f32[5,128]{0,1:T(8,128)S(1)} %bitcast.260), channel_id=1, source_target_pairs={{1,0},{2,1},{3,2},{4,3},{5,4},{6,5},{7,6},{8,7},{9,8},{10,9},{11,1... | collective-permute-start | bytes 7688 | tf_op jit(solution)/shard_map/ppermute | solution.py:23
  14.7 8.6 collective-permute-start.1
  89.6 301.4 %copy-start.12 = (f32[3,256]{1,0:T(4,128)S(1)}, f32[3,256]{1,0:T(4,128)}, u32[]{:S(2)}) copy-start(f32[3,256]{1,0:T(4,128)} %param.38) | copy-start | bytes 9220
  391.1 11.0 %copy-start.10 = (s32[256,32]{0,1:T(8,128)S(1)}, s32[256,32]{0,1:T(8,128)}, u32[]{:S(2)}) copy-start(s32[256,32]{0,1:T(8,128)} %param.42) | copy-start | bytes 98308
  393.9 6.9 collective-permute-start.8
  395.2 6.8 collective-permute-start.7
  430.2 5.9 copy-start.6
  440.0 7.5 collective-permute-start.10
  441.3 7.4 collective-permute-start.9
  448.8 45.7 %copy-start.14 = (bf16[256,256]{1,0:T(8,128)(2,1)S(1)}, bf16[256,256]{1,0:T(8,128)(2,1)}, u32[]{:S(2)}) copy-start(bf16[256,256]{1,0:T(8,128)(2,1)} %param.41) | copy-start | bytes 393220
  448.8 45.7 %copy-start.22 = (f32[256]{0:T(256)S(1)}, f32[256]{0:T(256)}, u32[]{:S(2)}) copy-start(f32[256]{0:T(256)} %param.50) | copy-start | bytes 3076
  448.8 45.8 %copy-start.13 = (bf16[2,256,256]{2,1,0:T(8,128)(2,1)S(1)}, bf16[2,256,256]{2,1,0:T(8,128)(2,1)}, u32[]{:S(2)}) copy-start(bf16[2,256,256]{2,1,0:T(8,128)(2,1)} %param.48) | copy-start | bytes 786436
  477.0 4.8 copy-start.3
  477.0 5.9 copy-start.7
  486.8 17.9 %collective-permute-start.12 = (f32[3,128]{0,1:T(8,128)S(1)}, f32[3,128]{0,1:T(8,128)S(1)}, u32[]{:S(2)}, u32[]{:S(2)}) collective-permute-start(f32[3,128]{0,1:T(8,128)S(1)} %bitcast.263), channel_id=1, source_target_pairs={{1,0},{2,1},{3,2},{4,3},{5,4},{6,5},{7,6},{8,7},{9,8},{10,9},{11,1... | collective-permute-start | bytes 4616 | tf_op jit(solution)/shard_map/ppermute | solution.py:23
  488.1 16.7 %collective-permute-start.11 = (f32[3,128]{0,1:T(8,128)S(1)}, f32[3,128]{0,1:T(8,128)S(1)}, u32[]{:S(2)}, u32[]{:S(2)}) collective-permute-start(f32[3,128]{0,1:T(8,128)S(1)} %bitcast.262), channel_id=1, source_target_pairs={{0,1},{1,2},{2,3},{3,4},{4,5},{5,6},{6,7},{7,8},{8,9},{9,10},{10,1... | collective-permute-start | bytes 4616 | tf_op jit(solution)/shard_map/ppermute | solution.py:20
  496.6 55.3 %collective-permute-start.4 = (bf16[128,256]{1,0:T(8,128)(2,1)S(1)}, bf16[128,256]{1,0:T(8,128)(2,1)S(1)}, u32[]{:S(2)}, u32[]{:S(2)}) collective-permute-start(bf16[128,256]{1,0:T(8,128)(2,1)S(1)} %gather_fusion.11), channel_id=1, source_target_pairs={{1,0},{2,1},{3,2},{4,3},{5,4},{6,5},{7,6},{8,7},{9,8},{10,9},{11,1... | collective-permute-start | bytes 196616 | tf_op jit(solution)/shard_map/ppermute | solution.py:23
  497.9 54.0 %collective-permute-start.3 = (bf16[128,256]{1,0:T(8,128)(2,1)S(1)}, bf16[128,256]{1,0:T(8,128)(2,1)S(1)}, u32[]{:S(2)}, u32[]{:S(2)}) collective-permute-start(bf16[128,256]{1,0:T(8,128)(2,1)S(1)} %gather_fusion.10), channel_id=1, source_target_pairs={{0,1},{1,2},{2,3},{3,4},{4,5},{5,6},{6,7},{7,8},{8,9},{9,10},{10,1... | collective-permute-start | bytes 196616 | tf_op jit(solution)/shard_map/ppermute | solution.py:20
  504.9 47.2 %copy-start.15 = (bf16[2,2,64,64]{3,2,1,0:T(8,128)(2,1)S(1)}, bf16[2,2,64,64]{3,2,1,0:T(8,128)(2,1)}, u32[]{:S(2)}) copy-start(bf16[2,2,64,64]{3,2,1,0:T(8,128)(2,1)} %param.46) | copy-start | bytes 98308
  504.9 47.2 %copy-start.16 = (bf16[2,64,256]{2,1,0:T(8,128)(2,1)S(1)}, bf16[2,64,256]{2,1,0:T(8,128)(2,1)}, u32[]{:S(2)}) copy-start(bf16[2,64,256]{2,1,0:T(8,128)(2,1)} %param.47) | copy-start | bytes 196612
  504.9 47.2 %copy-start.19 = (bf16[2,8,64]{2,1,0:T(8,128)(2,1)S(1)}, bf16[2,8,64]{2,1,0:T(8,128)(2,1)}, u32[]{:S(2)}) copy-start(bf16[2,8,64]{2,1,0:T(8,128)(2,1)} %param.45) | copy-start | bytes 6148
  533.0 4.8 copy-start.4
  533.0 5.9 copy-start.8
  542.8 7.9 collective-permute-start.14
  544.1 7.7 collective-permute-start.13
  553.9 44.4 %collective-permute-start.6 = (bf16[128,256]{1,0:T(8,128)(2,1)S(1)}, bf16[128,256]{1,0:T(8,128)(2,1)S(1)}, u32[]{:S(2)}, u32[]{:S(2)}) collective-permute-start(bf16[128,256]{1,0:T(8,128)(2,1)S(1)} %gather_fusion.13), channel_id=1, source_target_pairs={{1,0},{2,1},{3,2},{4,3},{5,4},{6,5},{7,6},{8,7},{9,8},{10,9},{11,1... | collective-permute-start | bytes 196616 | tf_op jit(solution)/shard_map/ppermute | solution.py:23
  555.2 43.1 %collective-permute-start.5 = (bf16[128,256]{1,0:T(8,128)(2,1)S(1)}, bf16[128,256]{1,0:T(8,128)(2,1)S(1)}, u32[]{:S(2)}, u32[]{:S(2)}) collective-permute-start(bf16[128,256]{1,0:T(8,128)(2,1)S(1)} %gather_fusion.12), channel_id=1, source_target_pairs={{0,1},{1,2},{2,3},{3,4},{4,5},{5,6},{6,7},{7,8},{8,9},{9,10},{10,1... | collective-permute-start | bytes 196616 | tf_op jit(solution)/shard_map/ppermute | solution.py:20
  589.7 5.9 copy-start.9
  864.8 6.0 collective-permute-start.15
  (8 other events, 19.4 us)
Sparse Core Ops, SparseCore 0:
  602.7 261.3 all-reduce.1
where the time goes:
time: 879 us; the launch traced here: 878 us
  blocking collectives  296 us (34%)
  waiting for transfers between devices  265 us (30%)
  local copies, waits for them, and re-layouts  195 us (22%)
  starting transfers between devices  60.5 us (7%)
  other arithmetic  45.1 us (5%)
  between operations  14.8 us (2%)
    all_gather x1, blocking collectives, local(): others = lax.all_gather(partner, ('dom', 'sub'), axis=1, tiled=True)  296 us
    psum x1, waiting for transfers between devices, local(): total = lax.psum(scattered, ('dom', 'sub'))  262 us
    gather x4, local copies, waits for them, and re-layouts, local(): t[:, slot_major]  112 us
    ppermute x7, starting transfers between devices, with_halo(): lax.ppermute(lax.slice_in_dim(block, block.shape[dim] - width, None, axis...  43 us
    gather x2, local copies, waits for them, and re-layouts, local(): site_table[3][slot_major]  32.9 us
    gather x1, local copies, waits for them, and re-layouts, local(): offset = positions[:, None, :] - site_table[:3][:, slot_major]  27.9 us
    reduce_sum x5, other arithmetic, slot_field(): projected = jnp.sum(offset * source_dipole, axis=0)  23.5 us
  transfers between devices with their start and end apart: 17, of which 5 were waited for; matrix products, arithmetic and copies ran while one was open for 17% of the time, Pallas kernels for 0%

commit v1 on v0

--- a/solution.py
+++ b/solution.py
@@ -128,6 +128,14 @@
     field_gain,
     readout,
 ):
+
+    def use_zone(x_in):
+        peer_axis = "dom"
+        across = "sub"
+        for idx in (across, peer_axis):
+            x_in = lax.psum(x_in, idx)
+        return x_in
+
     rim_width = send_rows.shape[1]
     row_count = positions.shape[1]
     block_width = BLOCK
@@ -215,7 +223,7 @@
         .add(response_term.reshape(3, listed_count, block_width))
         .reshape(3, -1)
     )
-    total = lax.psum(scattered, ("dom", "sub"))
+    total = use_zone(scattered)
     own_share = lax.dynamic_slice_in_dim(total, domain_index * row_count, row_count, 1)
     response = partner_2(own_share, "grp", 0)
     return (site_result, response)

time: 879 us -> 1310 us (1.49)
  waiting for transfers between devices: 265 us -> 656 us
  starting transfers between devices: 60.5 us -> 98.6 us
    psum x1 -> x2, waiting for transfers between devices: 262 us -> 652 us  [use_zone(): x_in = lax.psum(x_in, idx)]
    ppermute x2, starting transfers between devices: 8.43 us -> 46.5 us  [partner_2(): return lax.ppermute(value, axis, pairs)]
  transfers between devices with their start and end apart: 17 -> 18, of which waited for: 5 -> 6; matrix products, arithmetic and copies ran while one was open for 17% -> 11% of each run, Pallas kernels for 0% -> 0%
where the time goes in v1:
time: 1310 us
  waiting for transfers between devices  656 us (50%)
  blocking collectives  296 us (23%)
  local copies, waits for them, and re-layouts  195 us (15%)
  starting transfers between devices  98.6 us (8%)
  other arithmetic  45.1 us (3%)
  between operations  14.8 us (1%)
    psum x2, waiting for transfers between devices, use_zone(): x_in = lax.psum(x_in, idx)  652 us
    all_gather x1, blocking collectives, local(): others = lax.all_gather(partner, ('dom', 'sub'), axis=1, tiled=True)  296 us
    gather x4, local copies, waits for them, and re-layouts, local(): t[:, slot_major]  112 us
    ppermute x2, starting transfers between devices, partner_2(): return lax.ppermute(value, axis, pairs)  46.5 us
    ppermute x7, starting transfers between devices, with_halo(): lax.ppermute(lax.slice_in_dim(block, block.shape[dim] - width, None, axis...  43 us
    gather x2, local copies, waits for them, and re-layouts, local(): site_table[3][slot_major]  32.9 us
    gather x1, local copies, waits for them, and re-layouts, local(): offset = positions[:, None, :] - site_table[:3][:, slot_major]  27.9 us
  transfers between devices with their start and end apart: 18, of which 6 were waited for; matrix products, arithmetic and copies ran while one was open for 11% of the time, Pallas kernels for 0%

profile of v1, /device:TPU:1, one launch (start us, length us, event | category | flops | bytes accessed | tf_op | source)
XLA Modules:
  0.0 1307.1 jit_solution(15734483733312606255)
XLA Ops:
  8.0 3.2 collective-permute-start
  14.7 5.5 collective-permute-start.1
  24.2 32.9 %gather_fusion.14 = f32[8192]{0:T(1024)S(1)} fusion(f32[513]{0:T(1024)S(1)} %slice_reduce_fusion, s32[8192]{0:T(1024)S(1)} %broadcast_clamp_fusion.4), kind=kCustom, calls=%fused_computation.14 | custom fusion | bytes 98304 | tf_op jit(solution)/shard_map/gather | solution.py:199
  57.2 27.9 %gather_fusion.9 = f32[8192,3]{1,0:T(8,128)} fusion(f32[3,513]{0,1:T(8,128)S(1)} %copy.124, s32[8192]{0:T(1024)S(1)} %broadcast_clamp_fusion.4), kind=kCustom, calls=%fused_computation.9 | custom fusion | bytes 229376 | tf_op jit(solution)/shard_map/gather | solution.py:157
  85.1 4.5 multiply_reduce_fusion.4
  91.5 2.5 subtract_reduce_fusion.4
  94.0 296.4 %all_gather.3 = f32[5,32768]{1,0:T(8,128)S(1)} all-gather(f32[5,256]{1,0:T(8,128)S(1)} %collective-permute-done), channel_id=1, replica_groups=mesh['grp'=2,'dom'=64,'sub'=2] {'dom','sub'}, dimensions={1}, use_global_device_ids=true | all-gather | bytes 660480 | tf_op jit(solution)/shard_map/all_gather | solution.py:154
  395.2 5.5 collective-permute-start.7
  402.1 36.6 %conditional.12 = (f32[3,256]{0,1:T(8,128)S(1)}) conditional(s32[]{:T(128)} %convert_element_type.76, (f32[256]{0:T(256)S(1)}, f32[32,256]{1,0:T(8,128)S(1)}, s32[32,256]{1,0:T(8,128)S(1)}, f32[3,513]{1,0:T(4,128)S(1)}, f32[3,32,256]{0,2,1:T(8,128)}, /*index=5*/f32[3,256]{0,1:T(8,128)S(1)}) %tuple.227, f32[3,256]{0,1:T(8,128)S(1)} %get-tuple-element.543), branch_computations={%region_23.26_spmd, %region_26.27_spmd} | conditional | flops 238336 | bytes 1860696 | solution.py:206
  402.3 27.9 %gather_fusion = f32[8192,3]{1,0:T(8,128)} fusion(f32[3,513]{0,1:T(8,128)S(1)} %copy.129, s32[8192]{0:T(1024)S(1)} %broadcast_clamp_fusion), kind=kCustom, calls=%fused_computation.2 | custom fusion | bytes 229376 | tf_op jit(solution)/shard_map/cond/branch_0_fun/gather | solution.py:211
  430.2 4.8 multiply_reduce_fusion
  436.1 2.5 subtract_reduce_fusion
  441.3 6.1 collective-permute-start.9
  448.9 36.7 %conditional.13 = (f32[3,256]{0,1:T(8,128)S(1)}) conditional(s32[]{:T(128)} %convert_element_type.76, (f32[256]{0:T(256)S(1)}, f32[32,256]{1,0:T(8,128)S(1)}, s32[32,256]{1,0:T(8,128)S(1)}, f32[3,513]{1,0:T(4,128)S(1)}, f32[3,32,256]{0,2,1:T(8,128)}, /*index=5*/f32[3,256]{0,1:T(8,128)S(1)}) %tuple.228, f32[3,256]{0,1:T(8,128)S(1)} %get-tuple-element.898), branch_computations={%region_27.30_spmd, %region_30.31_spmd} | conditional | flops 238336 | bytes 1860696 | solution.py:206
  449.1 27.9 %gather_fusion.1 = f32[8192,3]{1,0:T(8,128)} fusion(f32[3,513]{0,1:T(8,128)S(1)} %copy.133, s32[8192]{0:T(1024)S(1)} %broadcast_clamp_fusion.1), kind=kCustom, calls=%fused_computation.3 | custom fusion | bytes 229376 | tf_op jit(solution)/shard_map/cond/branch_0_fun/gather | solution.py:211
  477.0 4.8 multiply_reduce_fusion.1
  482.9 2.5 subtract_reduce_fusion.1
  488.1 6.4 collective-permute-start.11
  497.9 6.7 collective-permute-start.3
  504.9 36.6 %conditional.14 = (f32[3,256]{0,1:T(8,128)S(1)}) conditional(s32[]{:T(128)} %convert_element_type.76, (f32[256]{0:T(256)S(1)}, f32[32,256]{1,0:T(8,128)S(1)}, s32[32,256]{1,0:T(8,128)S(1)}, f32[3,513]{1,0:T(4,128)S(1)}, f32[3,32,256]{0,2,1:T(8,128)}, /*index=5*/f32[3,256]{0,1:T(8,128)S(1)}) %tuple.229, f32[3,256]{0,1:T(8,128)S(1)} %get-tuple-element.899), branch_computations={%region_31.34_spmd, %region_34.35_spmd} | conditional | flops 238336 | bytes 1860696 | solution.py:206
  505.1 27.9 %gather_fusion.2 = f32[8192,3]{1,0:T(8,128)} fusion(f32[3,513]{0,1:T(8,128)S(1)} %copy.137, s32[8192]{0:T(1024)S(1)} %broadcast_clamp_fusion.2), kind=kCustom, calls=%fused_computation.4 | custom fusion | bytes 229376 | tf_op jit(solution)/shard_map/cond/branch_0_fun/gather | solution.py:211
  533.0 4.8 multiply_reduce_fusion.2
  538.9 2.5 subtract_reduce_fusion.2
  544.1 6.4 collective-permute-start.13
  555.2 6.4 collective-permute-start.5
  561.6 36.6 %conditional.15 = (f32[3,256]{0,1:T(8,128)S(1)}) conditional(s32[]{:T(128)} %convert_element_type.76, (f32[256]{0:T(256)S(1)}, f32[32,256]{1,0:T(8,128)S(1)}, s32[32,256]{1,0:T(8,128)S(1)}, f32[3,513]{1,0:T(4,128)S(1)}, f32[3,32,256]{0,2,1:T(8,128)}, /*index=5*/f32[3,256]{0,1:T(8,128)S(1)}) %tuple.230, f32[3,256]{0,1:T(8,128)S(1)} %get-tuple-element.900), branch_computations={%region_35.38_spmd, %region_38.39_spmd} | conditional | flops 238336 | bytes 1860696 | solution.py:206
  561.8 27.9 %gather_fusion.3 = f32[8192,3]{1,0:T(8,128)} fusion(f32[3,513]{0,1:T(8,128)S(1)} %copy.141, s32[8192]{0:T(1024)S(1)} %broadcast_clamp_fusion.3), kind=kCustom, calls=%fused_computation.5 | custom fusion | bytes 229376 | tf_op jit(solution)/shard_map/cond/branch_0_fun/gather | solution.py:211
  589.7 4.8 multiply_reduce_fusion.3
  595.6 2.5 subtract_reduce_fusion.3
  602.6 91.5 %all-reduce.3.cloned.1.call-done = f32[3,32768]{1,0:T(4,128)} async-done(((f32[3,32768]{1,0:T(4,128)}), f32[3,32768]{1,0:T(4,128)}) %all-reduce.3.cloned.1.call-update) | async-done | bytes 393232 | tf_op jit(solution)/shard_map/psum | solution.py:136
  694.1 560.8 %all-reduce.5.cloned.1.call-done = f32[3,32768]{1,0:T(4,128)} async-done(((f32[3,32768]{1,0:T(4,128)}), f32[3,32768]{1,0:T(4,128)}) %all-reduce.5.cloned.1.call-update) | async-done | bytes 393232 | tf_op jit(solution)/shard_map/psum | solution.py:136
  1255.6 43.3 %collective-permute-start.15 = (f32[3,256]{1,0:T(4,128)S(1)}, f32[3,256]{1,0:T(4,128)S(1)}, u32[]{:S(2)}, u32[]{:S(2)}) collective-permute-start(f32[3,256]{1,0:T(4,128)S(1)} %constant_dynamic-slice_fusion), channel_id=1, source_target_pairs={{0,128},{128,0},{1,129},{129,1},{2,130},{130,2},{3,131},{131,3},{4... | collective-permute-start | bytes 9224 | tf_op jit(solution)/shard_map/ppermute | solution.py:31
  (213 shorter events, 48.5 us)
Async XLA Ops:
  7.2 591.5 %copy-start = (bf16[256,2]{0,1:T(2,128)(2,1)S(1)}, bf16[256,2]{0,1:T(2,128)(2,1)}, u32[]{:S(2)}) copy-start(bf16[256,2]{0,1:T(2,128)(2,1)} %param.51) | copy-start | bytes 3076
  7.2 686.9 %all-reduce.3.cloned.1.call-start = ((), (), s32[]{:S(2)}) async-start(), calls=%async_computation | async-start | bytes 1048576 | tf_op jit(solution)/shard_map/psum | solution.py:136
  8.0 86.1 %collective-permute-start = (f32[5,256]{1,0:T(8,128)S(1)}, f32[5,256]{1,0:T(8,128)S(1)}, u32[]{:S(2)}, u32[]{:S(2)}) collective-permute-start(f32[5,256]{1,0:T(8,128)S(1)} %pad_maximum_fusion), channel_id=1, source_target_pairs={{0,128},{128,0},{1,129},{129,1},{2,130},{130,2},{3,131},{131,3},{4... | collective-permute-start | bytes 15368 | tf_op jit(solution)/shard_map/ppermute | solution.py:31
  12.8 10.5 collective-permute-start.2
  14.7 8.6 collective-permute-start.1
  89.6 301.4 %copy-start.12 = (f32[3,256]{1,0:T(4,128)S(1)}, f32[3,256]{1,0:T(4,128)}, u32[]{:S(2)}) copy-start(f32[3,256]{1,0:T(4,128)} %param.38) | copy-start | bytes 9220
  391.1 11.0 copy-start.10
  393.9 6.9 collective-permute-start.8
  395.2 6.8 collective-permute-start.7
  430.2 5.9 copy-start.6
  440.0 7.5 collective-permute-start.10
  441.3 7.4 collective-permute-start.9
  448.8 45.7 %copy-start.14 = (bf16[256,256]{1,0:T(8,128)(2,1)S(1)}, bf16[256,256]{1,0:T(8,128)(2,1)}, u32[]{:S(2)}) copy-start(bf16[256,256]{1,0:T(8,128)(2,1)} %param.41) | copy-start | bytes 393220
  448.8 45.7 %copy-start.22 = (f32[256]{0:T(256)S(1)}, f32[256]{0:T(256)}, u32[]{:S(2)}) copy-start(f32[256]{0:T(256)} %param.50) | copy-start | bytes 3076
  448.8 45.8 %copy-start.13 = (bf16[2,256,256]{2,1,0:T(8,128)(2,1)S(1)}, bf16[2,256,256]{2,1,0:T(8,128)(2,1)}, u32[]{:S(2)}) copy-start(bf16[2,256,256]{2,1,0:T(8,128)(2,1)} %param.48) | copy-start | bytes 786436
  477.0 4.8 copy-start.3
  477.0 5.9 copy-start.7
  486.8 17.9 %collective-permute-start.12 = (f32[3,128]{0,1:T(8,128)S(1)}, f32[3,128]{0,1:T(8,128)S(1)}, u32[]{:S(2)}, u32[]{:S(2)}) collective-permute-start(f32[3,128]{0,1:T(8,128)S(1)} %bitcast.263), channel_id=1, source_target_pairs={{1,0},{2,1},{3,2},{4,3},{5,4},{6,5},{7,6},{8,7},{9,8},{10,9},{11,1... | collective-permute-start | bytes 4616 | tf_op jit(solution)/shard_map/ppermute | solution.py:23
  488.1 16.7 %collective-permute-start.11 = (f32[3,128]{0,1:T(8,128)S(1)}, f32[3,128]{0,1:T(8,128)S(1)}, u32[]{:S(2)}, u32[]{:S(2)}) collective-permute-start(f32[3,128]{0,1:T(8,128)S(1)} %bitcast.262), channel_id=1, source_target_pairs={{0,1},{1,2},{2,3},{3,4},{4,5},{5,6},{6,7},{7,8},{8,9},{9,10},{10,1... | collective-permute-start | bytes 4616 | tf_op jit(solution)/shard_map/ppermute | solution.py:20
  496.6 55.3 %collective-permute-start.4 = (bf16[128,256]{1,0:T(8,128)(2,1)S(1)}, bf16[128,256]{1,0:T(8,128)(2,1)S(1)}, u32[]{:S(2)}, u32[]{:S(2)}) collective-permute-start(bf16[128,256]{1,0:T(8,128)(2,1)S(1)} %gather_fusion.11), channel_id=1, source_target_pairs={{1,0},{2,1},{3,2},{4,3},{5,4},{6,5},{7,6},{8,7},{9,8},{10,9},{11,1... | collective-permute-start | bytes 196616 | tf_op jit(solution)/shard_map/ppermute | solution.py:23
  497.9 54.0 %collective-permute-start.3 = (bf16[128,256]{1,0:T(8,128)(2,1)S(1)}, bf16[128,256]{1,0:T(8,128)(2,1)S(1)}, u32[]{:S(2)}, u32[]{:S(2)}) collective-permute-start(bf16[128,256]{1,0:T(8,128)(2,1)S(1)} %gather_fusion.10), channel_id=1, source_target_pairs={{0,1},{1,2},{2,3},{3,4},{4,5},{5,6},{6,7},{7,8},{8,9},{9,10},{10,1... | collective-permute-start | bytes 196616 | tf_op jit(solution)/shard_map/ppermute | solution.py:20
  504.9 47.2 %copy-start.15 = (bf16[2,2,64,64]{3,2,1,0:T(8,128)(2,1)S(1)}, bf16[2,2,64,64]{3,2,1,0:T(8,128)(2,1)}, u32[]{:S(2)}) copy-start(bf16[2,2,64,64]{3,2,1,0:T(8,128)(2,1)} %param.46) | copy-start | bytes 98308
  504.9 47.2 %copy-start.16 = (bf16[2,64,256]{2,1,0:T(8,128)(2,1)S(1)}, bf16[2,64,256]{2,1,0:T(8,128)(2,1)}, u32[]{:S(2)}) copy-start(bf16[2,64,256]{2,1,0:T(8,128)(2,1)} %param.47) | copy-start | bytes 196612
  504.9 47.2 %copy-start.19 = (bf16[2,8,64]{2,1,0:T(8,128)(2,1)S(1)}, bf16[2,8,64]{2,1,0:T(8,128)(2,1)}, u32[]{:S(2)}) copy-start(bf16[2,8,64]{2,1,0:T(8,128)(2,1)} %param.45) | copy-start | bytes 6148
  533.0 5.9 copy-start.8
  542.8 7.9 collective-permute-start.14
  544.1 7.7 collective-permute-start.13
  553.9 44.4 %collective-permute-start.6 = (bf16[128,256]{1,0:T(8,128)(2,1)S(1)}, bf16[128,256]{1,0:T(8,128)(2,1)S(1)}, u32[]{:S(2)}, u32[]{:S(2)}) collective-permute-start(bf16[128,256]{1,0:T(8,128)(2,1)S(1)} %gather_fusion.13), channel_id=1, source_target_pairs={{1,0},{2,1},{3,2},{4,3},{5,4},{6,5},{7,6},{8,7},{9,8},{10,9},{11,1... | collective-permute-start | bytes 196616 | tf_op jit(solution)/shard_map/ppermute | solution.py:23
  555.2 43.1 %collective-permute-start.5 = (bf16[128,256]{1,0:T(8,128)(2,1)S(1)}, bf16[128,256]{1,0:T(8,128)(2,1)S(1)}, u32[]{:S(2)}, u32[]{:S(2)}) collective-permute-start(bf16[128,256]{1,0:T(8,128)(2,1)S(1)} %gather_fusion.12), channel_id=1, source_target_pairs={{0,1},{1,2},{2,3},{3,4},{4,5},{5,6},{6,7},{7,8},{8,9},{9,10},{10,1... | collective-permute-start | bytes 196616 | tf_op jit(solution)/shard_map/ppermute | solution.py:20
  589.7 5.9 copy-start.9
  602.5 652.4 %all-reduce.5.cloned.1.call-start = ((), (), s32[]{:S(2)}) async-start(), calls=%async_computation.1 | async-start | bytes 1048576 | tf_op jit(solution)/shard_map/psum | solution.py:136
  1255.6 44.1 %collective-permute-start.15 = (f32[3,256]{1,0:T(4,128)S(1)}, f32[3,256]{1,0:T(4,128)S(1)}, u32[]{:S(2)}, u32[]{:S(2)}) collective-permute-start(f32[3,256]{1,0:T(4,128)S(1)} %constant_dynamic-slice_fusion), channel_id=1, source_target_pairs={{0,128},{128,0},{1,129},{129,1},{2,130},{130,2},{3,131},{131,3},{4... | collective-permute-start | bytes 9224 | tf_op jit(solution)/shard_map/ppermute | solution.py:31
  (9 other events, 24.1 us)
Sparse Core Ops, SparseCore 0:
  602.7 91.3 all-reduce.2
  696.9 558.0 all-reduce.4
